TPU v7x, 32 devices: a whole 2x2x4 slice. The times are simulated.
32 devices in a mesh: groups: 2 (over x), tensor: 16 (over z, y, core).
Axes of the slice: x: 2, y: 2, z: 4, core: 2. Of those that a mesh axis runs over, the one named last changes fastest.
Arguments:
- residual_in: bfloat16 [1024, 6144], P('groups', 'tensor'), parts along dimension 0
- norm_gain: bfloat16 [6144], P('tensor'), may hold values from 0.099609375 to 1.8984375
- final_gain: bfloat16 [6144], P('tensor'), may hold values from 0.099609375 to 1.8984375
- expert_ids: int32 [1024, 2], P('groups'), parts along dimension 0, may hold values from 0 to 3, all different within a row; in each aligned block of 512 rows (0 to 511, 512 to 1023, ...) at most 384 rows name the same one
- gate_values: float32 [1024, 2], P('groups'), parts along dimension 0, may hold values from 0.2 to 1
- w_gate: bfloat16 [6144, 32768], P(None, 'tensor'), may hold values from -0.078125 to 0.078125
- w_up: bfloat16 [6144, 32768], P(None, 'tensor'), may hold values from -0.078125 to 0.078125
- w_down: bfloat16 [32768, 6144], P('tensor')
- lm_head: bfloat16 [6144, 32768], P(None, 'tensor')
- target_ids: int32 [1024], P('groups'), parts along dimension 0, may hold values from 0 to 32767
- lengths: int32 [16], P('groups'), parts along dimension 0, may hold values from 1 to 64
Outputs:
- masked_logprob: float32 [1024], P(('groups', 'tensor')), parts along dimension 0
There are 2 independent parts, one for each index of `groups`. A program takes and returns all parts, laid end to end along the dimension named above; an argument that names none is the same for every part. Nothing has to cross between parts.
Inputs may be any that keep to these rules, and one draw needn't show every extreme that they name: `expert_ids`: no expert is named by more than 384 tokens of a frontier batch, a bound that some block reaches.
All inputs are finite; a program needn't handle non-finite values.
Results may differ from a plain program's by a relative error of at most 0.0055.
Values may be sent and summed in bfloat16 or wider, within the bound.
No kernel may reach another device: no remote copies, remote signals or barrier semaphores. Data moves between devices by JAX's collectives and lax.ppermute only.
A program may use at most 192 MiB of HBM per device.

v0:
```python
import jax
import jax.numpy as jnp
from jax import lax
from jax.sharding import PartitionSpec as P

D = 6144
EXPERTS = 4
EXP_FF = 8192
TOP = 2
SEQ = 64
CAP = 384
epsilon = 1e-05


def combined_all(array, axis, combine):
    everything = jax.tree.map(lambda part: lax.all_gather(part, axis), array)
    leading = jax.tree.map(lambda part: part[0], everything)

    def hop(k, so_far):
        return combine(so_far, jax.tree.map(lambda part: part[k], everything))

    return lax.fori_loop(1, lax.axis_size(axis), hop, leading)


def slots_of(expert_ids):
    flat_ids = expert_ids.reshape(-1)
    pairs = jnp.arange(flat_ids.shape[0], dtype=jnp.int32)
    before = (pairs[None, :] < pairs[:, None]) & (flat_ids[None, :] == flat_ids[:, None])
    return jnp.sum(before.astype(jnp.int32), axis=1).reshape(expert_ids.shape)


def slot_tokens(expert_ids, slot_index):
    slot_code = (expert_ids * CAP + slot_index).reshape(-1)
    owner = jnp.arange(slot_code.shape[0], dtype=jnp.int32) // TOP
    wanted = jnp.arange(EXPERTS * CAP, dtype=jnp.int32)
    matches = slot_code[None, :] == wanted[:, None]
    return jnp.sum(jnp.where(matches, owner[None, :] + 1, 0), axis=1) - 1


def normalize(values, squares_total, gain_vec):
    return (
        values / jnp.sqrt(squares_total[:, None] / D + epsilon) * gain_vec.astype(jnp.float32)
    ).astype(jnp.bfloat16)


def body(
    residual_in,
    norm_gain,
    final_gain,
    expert_ids,
    gate_values,
    w_gate,
    w_up,
    w_down,
    lm_head,
    target_ids,
    lengths,
):
    tokens, feature_cols = residual_in.shape
    hidden_dev = w_gate.shape[1]
    per_expert = EXP_FF // hidden_dev
    expert_now = lax.axis_index("tensor") // per_expert
    stream = residual_in.astype(jnp.float32)
    in_total = lax.psum(jnp.sum(stream * stream, axis=1), "tensor")
    normed = normalize(stream, in_total, norm_gain)
    slot_index = slots_of(expert_ids)
    token_of = slot_tokens(expert_ids, slot_index)
    zero_bf = jnp.zeros((), jnp.bfloat16)
    own_slots = lax.dynamic_slice_in_dim(token_of, expert_now * CAP, CAP)
    occupied = own_slots >= 0
    safe_index = jnp.maximum(own_slots, 0)
    slot_rows = jnp.where(
        occupied[:, None], lax.all_gather(normed, "tensor", axis=1, tiled=True)[safe_index], zero_bf
    )
    gate_out = jnp.dot(slot_rows, w_gate, preferred_element_type=jnp.float32)
    up_out = jnp.dot(slot_rows, w_up, preferred_element_type=jnp.float32)
    hidden = (jax.nn.silu(gate_out) * up_out).astype(jnp.bfloat16)
    partial_value = jnp.dot(hidden, w_down, preferred_element_type=jnp.float32)
    weight_own = jnp.where(expert_ids == expert_now, gate_values, jnp.zeros_like(gate_values))
    weighted = (
        weight_own[:, 0:1] * partial_value[slot_index[:, 0]]
        + weight_own[:, 1:2] * partial_value[slot_index[:, 1]]
    )
    moe_cols = lax.psum_scatter(weighted, "tensor", scatter_dimension=1, tiled=True)
    mixture = stream + moe_cols
    out_total = lax.psum(jnp.sum(mixture * mixture, axis=1), "tensor")
    normed_out = normalize(mixture, out_total, final_gain)
    vocab_dev = lm_head.shape[1]
    logits = jnp.dot(
        lax.all_gather(normed_out, "tensor", axis=1, tiled=True),
        lm_head,
        preferred_element_type=jnp.float32,
    )
    row_max = jnp.max(logits, axis=1)
    row_total = jnp.sum(jnp.exp(logits - row_max[:, None]), axis=1)
    local_ids = target_ids - lax.axis_index("tensor") * vocab_dev
    vocab_cols = jnp.arange(vocab_dev, dtype=jnp.int32)
    picked = jnp.sum(jnp.where(vocab_cols[None, :] == local_ids[:, None], logits, 0.0), axis=1)

    def joined(earlier, later):
        merged_max = jnp.maximum(earlier[0], later[0])
        merged_total = earlier[1] * jnp.exp(earlier[0] - merged_max) + later[1] * jnp.exp(
            later[0] - merged_max
        )
        return (merged_max, merged_total, earlier[2] + later[2])

    merged_max, merged_total, target_logit = combined_all(
        (row_max, row_total, picked), "tensor", joined
    )
    logprob = target_logit - merged_max - jnp.log(merged_total)
    rows_dev = tokens // lax.axis_size("tensor")
    first_row = lax.axis_index("tensor") * rows_dev
    own_rows = lax.dynamic_slice_in_dim(logprob, first_row, rows_dev)
    position = first_row + jnp.arange(rows_dev, dtype=jnp.int32)
    in_length = position % SEQ < lengths[position // SEQ]
    return jnp.where(in_length, own_rows, jnp.zeros_like(own_rows)).astype(jnp.float32)


def solution(mesh):
    return jax.shard_map(
        body,
        mesh=mesh,
        in_specs=(
            P("groups", "tensor"),
            P("tensor"),
            P("tensor"),
            P("groups", None),
            P("groups", None),
            P(None, "tensor"),
            P(None, "tensor"),
            P("tensor", None),
            P(None, "tensor"),
            P("groups"),
            P("groups"),
        ),
        out_specs=P(("groups", "tensor")),
        check_vma=False,
    )
```

profile of v0, /device:TPU:0, one launch (start us, length us, event | category | flops | bytes accessed | tf_op | source)
XLA Modules:
  0.0 534.1 jit_solution(18296530312608750279)
XLA Ops:
  6.5 0.0 copy-start
  6.5 0.0 all-gather.9.cloned.1.call-start
  6.5 1.2 fusion.4
  7.7 34.9 %psum.14 = f32[512]{0:T(512)S(1)} all-reduce(f32[512]{0:T(512)S(1)} %fusion.4), channel_id=1, replica_groups=mesh['groups'=2,'tensor'=16] {'tensor'}, use_global_device_ids=true, to_apply=%region_3.4 | all-reduce | flops 512 | bytes 4096 | tf_op jit(solution)/shard_map/psum | solution.py:64
  42.6 0.7 convert_element_type.23
  43.3 1.9 fusion.6
  45.3 0.0 all-gather.9.cloned.1.call-update
  45.3 0.0 reduce-scatter.2.cloned.1.call-start
  45.4 0.8 copy.24
  46.2 0.2 eq.53
  46.4 0.5 convert_reduce_fusion
  46.9 0.2 reshape.95
  47.1 0.1 copy.25
  47.2 0.7 multiply_add_fusion.2
  47.9 0.1 copy.26
  48.1 0.2 eq.57
  48.3 0.7 select_reduce_fusion
  49.0 0.1 fusion.13
  49.1 0.1 fusion.14
  49.1 0.3 fusion.7
  49.5 0.7 compare_select_fusion.2
  50.2 58.2 %all-gather.9.cloned.1.call-done = bf16[512,6144]{1,0:T(8,128)(2,1)} async-done(((bf16[512,384]{1,0:T(8,128)(2,1)}), bf16[512,6144]{1,0:T(8,128)(2,1)}) %all-gather.9.cloned.1.call-update) | async-done | bytes 6291472 | tf_op jit(solution)/shard_map/all_gather | solution.py:73
  108.4 15.5 %gather_fusion.1 = bf16[384,6144]{1,0:T(8,128)(2,1)} fusion(bf16[512,6144]{1,0:T(8,128)(2,1)} %all-gather.9.cloned.1.call-done, s32[1024]{0:T(1024)S(1)} %pad_clamp_fusion.2), kind=kCustom, calls=%fused_computation.1 | custom fusion | bytes 9438720 | tf_op jit(solution)/shard_map/gather | solution.py:73
  123.9 0.0 copy-start.2
  123.9 16.5 %fusion.2 = f32[384,2048]{1,0:T(8,128)S(1)} fusion(bf16[6144,2048]{1,0:T(8,128)(2,1)} %param.18, bf16[384,6144]{1,0:T(8,128)(2,1)} %gather_fusion.1, pred[384]{0:T(512)(128)(4,1)S(1)} %fusion.13), kind=kOutput, calls=%fused_computation.20 | convolution fusion | flops 9666035712 | bytes 33030528 | tf_op jit(solution)/shard_map/dot_general | solution.py:75
  140.4 0.0 copy-done.2
  140.4 15.2 %multiply_convert_fusion.clone.4 = bf16[384,2048]{1,0:T(8,128)(2,1)S(1)} fusion(f32[384,2048]{1,0:T(8,128)S(1)} %fusion.2, bf16[6144,2048]{1,0:T(8,128)(2,1)} %param.19, bf16[384,6144]{1,0:T(8,128)(2,1)S(1)} %copy-done.2, pred[384]{0:T(512)(128)(4,1)S(1)} %fusion.13), kind=kOutput, calls=%fused_computation.18.clone.clone.clone.1 | convolution fusion | flops 9670754304 | bytes 34603392 | tf_op jit(solution)/shard_map/dot_general | solution.py:76
  155.6 17.2 %fusion.1 = f32[384,6144]{1,0:T(8,128)} fusion(bf16[2048,6144]{1,0:T(8,128)(2,1)} %param.20, bf16[384,2048]{1,0:T(8,128)(2,1)S(1)} %multiply_convert_fusion.clone.4), kind=kOutput, calls=%fused_computation.19 | convolution fusion | flops 9663676416 | bytes 36175872 | tf_op jit(solution)/shard_map/dot_general | solution.py:78
  172.8 16.3 %gather_fusion.2 = f32[512,6144]{1,0:T(8,128)} fusion(f32[384,6144]{1,0:T(8,128)} %fusion.1, s32[1024]{0:T(1024)S(1)} %get-tuple-element.213), kind=kCustom, calls=%fused_computation.2 | custom fusion | bytes 25167872 | tf_op jit(solution)/shard_map/gather | solution.py:81
  189.0 16.2 %gather_fusion.3 = f32[512,6144]{1,0:T(8,128)} fusion(f32[384,6144]{1,0:T(8,128)} %fusion.1, s32[1024]{0:T(1024)S(1)} %get-tuple-element.212), kind=kCustom, calls=%fused_computation.3 | custom fusion | bytes 25167872 | tf_op jit(solution)/shard_map/gather | solution.py:82
  205.2 14.0 %multiply_add_fusion.1 = f32[512,6144]{1,0:T(8,128)} fusion(f32[512,6144]{1,0:T(8,128)} %gather_fusion.3, f32[512,6144]{1,0:T(8,128)} %gather_fusion.2, f32[512]{0:T(512)S(1)} %bitcast.51, f32[512]{0:T(512)S(1)} %bitcast.50), kind=kLoop, calls=%fused_computation.8 | loop fusion | flops 9437184 | bytes 37752832 | tf_op jit(solution)/shard_map/add | solution.py:81
  219.2 0.0 copy-start.4
  219.2 0.0 copy-start.1
  219.2 0.0 copy-start.3
  219.2 0.0 reduce-scatter.2.cloned.1.call-update
  219.2 0.0 all-gather.11.cloned.1.call-start
  219.3 0.6 copy-done.4
  219.9 132.4 %reduce-scatter.2.cloned.1.call-done = f32[512,384]{1,0:T(8,128)} async-done(((f32[512,6144]{1,0:T(8,128)}), f32[512,384]{1,0:T(8,128)}) %reduce-scatter.2.cloned.1.call-update) | async-done | bytes 786448 | tf_op jit(solution)/shard_map/reduce_scatter | solution.py:84
  352.3 0.0 copy-done.1
  352.3 1.3 multiply_reduce_fusion
  353.6 31.6 %psum.15 = f32[512]{0:T(512)S(1)} all-reduce(f32[512]{0:T(512)S(1)} %multiply_reduce_fusion), channel_id=1, replica_groups=mesh['groups'=2,'tensor'=16] {'tensor'}, use_global_device_ids=true, to_apply=%region_6.7 | all-reduce | flops 512 | bytes 4096 | tf_op jit(solution)/shard_map/psum | solution.py:86
  385.2 2.1 multiply_convert_fusion.1
  387.3 0.0 all-gather.11.cloned.1.call-update
  387.4 0.0 copy-done
  387.4 0.7 gather_fusion
  388.1 0.0 copy-done.3
  388.1 62.3 %all-gather.11.cloned.1.call-done = bf16[512,6144]{1,0:T(8,128)(2,1)} async-done(((bf16[512,384]{1,0:T(8,128)(2,1)}), bf16[512,6144]{1,0:T(8,128)(2,1)}) %all-gather.11.cloned.1.call-update) | async-done | bytes 6291472 | tf_op jit(solution)/shard_map/all_gather | solution.py:90
  450.4 18.6 %fusion.22 = (f32[512]{0:T(512)S(1)}, f32[512,2048]{1,0:T(8,128)S(1)}) fusion(bf16[512,6144]{1,0:T(8,128)(2,1)} %all-gather.11.cloned.1.call-done, bf16[6144,2048]{1,0:T(8,128)(2,1)} %param.21), kind=kOutput, calls=%fused_computation.73 | convolution fusion | flops 12885950464 | bytes 35653632 | tf_op jit(solution)/shard_map/dot_general | solution.py:89
  469.0 1.4 select_reduce_fusion.1
  470.4 18.8 %all-gather.5 = f32[16,1,512]{2,1,0:T(1,128)S(1)} all-gather(f32[1,1,512]{2,1,0:T(1,128)S(1)} %bitcast.49), channel_id=4, replica_groups=mesh['groups'=2,'tensor'=16] {'tensor'}, dimensions={0}, use_global_device_ids=true | all-gather | bytes 34816 | tf_op jit(solution)/shard_map/all_gather | solution.py:16
  489.3 17.5 %all-gather.4 = f32[16,1,512]{2,1,0:T(1,128)S(1)} all-gather(f32[1,1,512]{2,1,0:T(1,128)S(1)} %bitcast.48), channel_id=3, replica_groups=mesh['groups'=2,'tensor'=16] {'tensor'}, dimensions={0}, use_global_device_ids=true | all-gather | bytes 34816 | tf_op jit(solution)/shard_map/all_gather | solution.py:16
  506.8 18.8 %all-gather.3 = f32[16,1,512]{2,1,0:T(1,128)S(1)} all-gather(f32[1,1,512]{2,1,0:T(1,128)S(1)} %bitcast.47), channel_id=2, replica_groups=mesh['groups'=2,'tensor'=16] {'tensor'}, dimensions={0}, use_global_device_ids=true | all-gather | bytes 34816 | tf_op jit(solution)/shard_map/all_gather | solution.py:16
  525.6 1.4 while.19
  527.0 0.6 compare_select_fusion.6
  (77 shorter events, 0.9 us)
Async XLA Ops:
  6.5 380.9 %copy-start = (s32[8]{0:T(128)S(1)}, s32[8]{0:T(128)}, u32[]{:S(2)}) copy-start(s32[8]{0:T(128)} %param.23) | copy-start | bytes 100
  6.5 101.9 %all-gather.9.cloned.1.call-start = ((), (), s32[]{:S(2)}) async-start(), calls=%async_computation.1 | async-start | bytes 6684672 | tf_op jit(solution)/shard_map/all_gather | solution.py:73
  45.3 307.0 %reduce-scatter.2.cloned.1.call-start = ((), (), s32[]{:S(2)}) async-start(), calls=%async_computation.2 | async-start | bytes 13369344 | tf_op jit(solution)/shard_map/reduce_scatter | solution.py:84
  123.9 16.5 %copy-start.2 = (bf16[384,6144]{1,0:T(8,128)(2,1)S(1)}, bf16[384,6144]{1,0:T(8,128)(2,1)}, u32[]{:S(2)}) copy-start(bf16[384,6144]{1,0:T(8,128)(2,1)} %gather_fusion.1) | copy-start | bytes 14155780
  219.2 0.7 copy-start.4
  219.2 133.1 %copy-start.1 = (bf16[512,384]{1,0:T(8,128)(2,1)S(1)}, bf16[512,384]{1,0:T(8,128)(2,1)}, u32[]{:S(2)}) copy-start(bf16[512,384]{1,0:T(8,128)(2,1)} %param.13) | copy-start | bytes 1179652
  219.2 168.9 %copy-start.3 = (s32[512]{0:T(512)S(1)}, s32[512]{0:T(512)}, u32[]{:S(2)}) copy-start(s32[512]{0:T(512)} %param.22) | copy-start | bytes 6148
  219.2 231.2 %all-gather.11.cloned.1.call-start = ((), (), s32[]{:S(2)}) async-start(), calls=%async_computation.3 | async-start | bytes 6684672 | tf_op jit(solution)/shard_map/all_gather | solution.py:90
Sparse Core Ops, SparseCore 0:
  45.4 62.9 all-gather.8
  219.4 132.9 reduce-scatter.1
  387.5 62.9 all-gather.10
where the time goes:
time: 535 us; the launch traced here: 534 us
  waiting for transfers between devices  253 us (47%)
  blocking collectives  122 us (23%)
  matrix products  67.5 us (13%)
  local copies, waits for them, and re-layouts  51.2 us (10%)
  other arithmetic  26.8 us (5%)
  between operations  13.3 us (2%)
    reduce_scatter x1, waiting for transfers between devices, body(): lax.psum_scatter(weighted, 'tensor', scatter_dimension=1, tiled=True)  132 us
    all_gather x1, waiting for transfers between devices, body(): lax.all_gather(normed_out, 'tensor', axis=1, tiled=True)  62.3 us
    all_gather x1, waiting for transfers between devices, body(): lax.all_gather(normed, 'tensor', axis=1, tiled=True)[safe_index]  58.2 us
    all_gather x3, blocking collectives, combined_all(): everything = jax.tree.map(lambda part: lax.all_gather(part, axis), array)  55.2 us
    psum x1, blocking collectives, body(): in_total = lax.psum(jnp.sum(stream * stream, axis=1), 'tensor')  34.9 us
    psum x1, blocking collectives, body(): out_total = lax.psum(jnp.sum(mixture * mixture, axis=1), 'tensor')  31.6 us
    dot_general x1, matrix products, body(): jnp.dot(lax.all_gather(normed_out, 'tensor', axis=1, tiled=True), lm_head...  18.6 us
    dot_general x1, matrix products, body(): partial_value = jnp.dot(hidden, w_down, preferred_element_type=jnp.float32)  17.2 us
  transfers between devices with their start and end apart: 3, of which 3 were waited for; matrix products, arithmetic and copies ran while one was open for 1% of the time, Pallas kernels for 0%

commit v1 on v0

--- a/solution.py
+++ b/solution.py
@@ -10,6 +10,33 @@
 SEQ = 64
 CAP = 384
 epsilon = 1e-05
+
+
+def roads_replace(here_x, at_axis):
+    net_axis = "tensor"
+    side_arr = lax.axis_size(net_axis)
+    formed = lax.axis_index(net_axis)
+    latest, e_next, work_now = (side_arr, formed, here_x.shape[at_axis])
+    big = jnp.zeros(
+        [nth * latest if d == at_axis else nth for d, nth in enumerate(here_x.shape)], here_x.dtype
+    )
+    piece_out = v_next = here_x
+    p = 1
+    taken_in = lax.dynamic_update_slice_in_dim(big, here_x, e_next * work_now, axis=at_axis)
+    while p < latest // 2 + 1:
+        piece_out = lax.ppermute(
+            piece_out, net_axis, [(d, (d + 1) % latest) for d in range(latest)]
+        )
+        taken_in = lax.dynamic_update_slice_in_dim(
+            taken_in, piece_out, (e_next - p) % latest * work_now, axis=at_axis
+        )
+        if 2 * p < latest:
+            v_next = lax.ppermute(v_next, net_axis, [(d, (d - 1) % latest) for d in range(latest)])
+            taken_in = lax.dynamic_update_slice_in_dim(
+                taken_in, v_next, (e_next + p) % latest * work_now, axis=at_axis
+            )
+        p += 1
+    return taken_in
 
 
 def combined_all(array, axis, combine):
@@ -86,11 +113,7 @@
     out_total = lax.psum(jnp.sum(mixture * mixture, axis=1), "tensor")
     normed_out = normalize(mixture, out_total, final_gain)
     vocab_dev = lm_head.shape[1]
-    logits = jnp.dot(
-        lax.all_gather(normed_out, "tensor", axis=1, tiled=True),
-        lm_head,
-        preferred_element_type=jnp.float32,
-    )
+    logits = jnp.dot(roads_replace(normed_out, 1), lm_head, preferred_element_type=jnp.float32)
     row_max = jnp.max(logits, axis=1)
     row_total = jnp.sum(jnp.exp(logits - row_max[:, None]), axis=1)
     local_ids = target_ids - lax.axis_index("tensor") * vocab_dev

time: 535 us -> 559 us (1.045)
  starting transfers between devices: 0.09 us -> 31.6 us
  waiting for transfers between devices: 253 us -> 226 us
  local copies, waits for them, and re-layouts: 51.2 us -> 67.7 us
    all_gather x1 -> x0, waiting for transfers between devices: 62.3 us -> none  [body(): lax.all_gather(normed_out, 'tensor', axis=1, tiled=True)]
    ppermute x0 -> x15, waiting for transfers between devices: none -> 35.8 us  [the longest x8 35.7 us: roads_replace(): lax.ppermute(piece_out, net_axis, [(d, (d + 1) % latest) for d in range(l...]
    ppermute x0 -> x15, starting transfers between devices: none -> 31.5 us  [the longest x7 22.1 us: roads_replace(): lax.ppermute(v_next, net_axis, [(d, (d - 1) % latest) for d in range(late...]
    dynamic_update_slice x0 -> x15, local copies, waits for them, and re-layouts: none -> 12.4 us  [the longest x8 6.64 us: roads_replace(): lax.dynamic_update_slice_in_dim(taken_in, piece_out, (e_next - p) % lates...]
  transfers between devices with their start and end apart: 3 -> 17, of which waited for: 3 -> 10; matrix products, arithmetic and copies ran while one was open for 1% -> 3% of each run, Pallas kernels for 0% -> 0%
where the time goes in v1:
time: 559 us; the launch traced here: 555 us
  waiting for transfers between devices  226 us (40%)
  blocking collectives  122 us (22%)
  local copies, waits for them, and re-layouts  67.7 us (12%)
  matrix products  67.7 us (12%)
  starting transfers between devices  31.6 us (6%)
  other arithmetic  25.8 us (5%)
  between operations  13.8 us (2%)
    reduce_scatter x1, waiting for transfers between devices, body(): lax.psum_scatter(weighted, 'tensor', scatter_dimension=1, tiled=True)  132 us
    all_gather x1, waiting for transfers between devices, body(): lax.all_gather(normed, 'tensor', axis=1, tiled=True)[safe_index]  58.2 us
    all_gather x3, blocking collectives, combined_all(): everything = jax.tree.map(lambda part: lax.all_gather(part, axis), array)  55.3 us
    ppermute x8, waiting for transfers between devices, roads_replace(): lax.ppermute(piece_out, net_axis, [(d, (d + 1) % latest) for d in range(l...  35.7 us
    psum x1, blocking collectives, body(): in_total = lax.psum(jnp.sum(stream * stream, axis=1), 'tensor')  34.9 us
    psum x1, blocking collectives, body(): out_total = lax.psum(jnp.sum(mixture * mixture, axis=1), 'tensor')  31.6 us
    ppermute x7, starting transfers between devices, roads_replace(): lax.ppermute(v_next, net_axis, [(d, (d - 1) % latest) for d in range(late...  22.1 us
    dot_general x1, matrix products, body(): jnp.dot(roads_replace(normed_out, 1), lm_head, preferred_element_type=jnp...  18.8 us
  transfers between devices with their start and end apart: 17, of which 10 were waited for; matrix products, arithmetic and copies ran while one was open for 3% of the time, Pallas kernels for 0%

profile of v1, /device:TPU:0, one launch (start us, length us, event | category | flops | bytes accessed | tf_op | source)
XLA Modules:
  0.0 555.4 jit_solution(1002991630882205076)
XLA Ops:
  6.5 1.2 fusion.4
  7.7 34.9 %psum.14 = f32[512]{0:T(512)S(1)} all-reduce(f32[512]{0:T(512)S(1)} %fusion.4), channel_id=1, replica_groups=mesh['groups'=2,'tensor'=16] {'tensor'}, use_global_device_ids=true, to_apply=%region_3.4 | all-reduce | flops 512 | bytes 4096 | tf_op jit(solution)/shard_map/psum | solution.py:91
  42.6 0.7 convert_element_type.23
  43.3 1.9 fusion.6
  45.3 0.8 copy.24
  47.2 0.7 multiply_add_fusion.2
  48.3 0.7 select_reduce_fusion
  49.5 0.7 compare_select_fusion.2
  50.2 58.2 %all-gather.8.cloned.1.call-done = bf16[512,6144]{1,0:T(8,128)(2,1)} async-done(((bf16[512,384]{1,0:T(8,128)(2,1)}), bf16[512,6144]{1,0:T(8,128)(2,1)}) %all-gather.8.cloned.1.call-update) | async-done | bytes 6291472 | tf_op jit(solution)/shard_map/all_gather | solution.py:100
  108.4 15.5 %gather_fusion.1 = bf16[384,6144]{1,0:T(8,128)(2,1)} fusion(bf16[512,6144]{1,0:T(8,128)(2,1)} %all-gather.8.cloned.1.call-done, s32[1024]{0:T(1024)S(1)} %pad_clamp_fusion.2), kind=kCustom, calls=%fused_computation.1 | custom fusion | bytes 9438720 | tf_op jit(solution)/shard_map/gather | solution.py:100
  123.9 16.5 %fusion.2 = f32[384,2048]{1,0:T(8,128)S(1)} fusion(bf16[6144,2048]{1,0:T(8,128)(2,1)} %param.18, bf16[384,6144]{1,0:T(8,128)(2,1)} %gather_fusion.1, pred[384]{0:T(512)(128)(4,1)S(1)} %fusion.13), kind=kOutput, calls=%fused_computation.20 | convolution fusion | flops 9666035712 | bytes 33030528 | tf_op jit(solution)/shard_map/dot_general | solution.py:102
  140.5 15.2 %multiply_convert_fusion.clone.4 = bf16[384,2048]{1,0:T(8,128)(2,1)S(1)} fusion(f32[384,2048]{1,0:T(8,128)S(1)} %fusion.2, bf16[6144,2048]{1,0:T(8,128)(2,1)} %param.19, bf16[384,6144]{1,0:T(8,128)(2,1)S(1)} %copy-done.2, pred[384]{0:T(512)(128)(4,1)S(1)} %fusion.13), kind=kOutput, calls=%fused_computation.18.clone.clone.clone.1 | convolution fusion | flops 9670754304 | bytes 34603392 | tf_op jit(solution)/shard_map/dot_general | solution.py:103
  155.7 17.2 %fusion.1 = f32[384,6144]{1,0:T(8,128)} fusion(bf16[2048,6144]{1,0:T(8,128)(2,1)} %param.20, bf16[384,2048]{1,0:T(8,128)(2,1)S(1)} %multiply_convert_fusion.clone.4), kind=kOutput, calls=%fused_computation.19 | convolution fusion | flops 9663676416 | bytes 36175872 | tf_op jit(solution)/shard_map/dot_general | solution.py:105
  172.9 16.3 %gather_fusion.2 = f32[512,6144]{1,0:T(8,128)} fusion(f32[384,6144]{1,0:T(8,128)} %fusion.1, s32[1024]{0:T(1024)S(1)} %get-tuple-element.215), kind=kCustom, calls=%fused_computation.2 | custom fusion | bytes 25167872 | tf_op jit(solution)/shard_map/gather | solution.py:108
  189.2 16.7 %gather_fusion.3 = f32[512,6144]{1,0:T(8,128)} fusion(f32[384,6144]{1,0:T(8,128)} %fusion.1, s32[1024]{0:T(1024)S(1)} %get-tuple-element.214), kind=kCustom, calls=%fused_computation.3 | custom fusion | bytes 25167872 | tf_op jit(solution)/shard_map/gather | solution.py:109
  205.9 14.0 %multiply_add_fusion.1 = f32[512,6144]{1,0:T(8,128)} fusion(f32[512,6144]{1,0:T(8,128)} %gather_fusion.3, f32[512,6144]{1,0:T(8,128)} %gather_fusion.2, f32[512]{0:T(512)S(1)} %bitcast.51, f32[512]{0:T(512)S(1)} %bitcast.50), kind=kLoop, calls=%fused_computation.8 | loop fusion | flops 9437184 | bytes 37752832 | tf_op jit(solution)/shard_map/add | solution.py:108
  219.9 0.6 copy-done.5
  220.6 132.5 %reduce-scatter.2.cloned.1.call-done = f32[512,384]{1,0:T(8,128)} async-done(((f32[512,6144]{1,0:T(8,128)}), f32[512,384]{1,0:T(8,128)}) %reduce-scatter.2.cloned.1.call-update) | async-done | bytes 786448 | tf_op jit(solution)/shard_map/reduce_scatter | solution.py:111
  353.0 1.4 multiply_reduce_fusion
  354.4 31.6 %psum.15 = f32[512]{0:T(512)S(1)} all-reduce(f32[512]{0:T(512)S(1)} %multiply_reduce_fusion), channel_id=1, replica_groups=mesh['groups'=2,'tensor'=16] {'tensor'}, use_global_device_ids=true, to_apply=%region_6.7 | all-reduce | flops 512 | bytes 4096 | tf_op jit(solution)/shard_map/psum | solution.py:113
  386.0 3.4 broadcast_in_dim.36
  389.5 1.0 constant_dynamic-update-slice_fusion.15
  390.4 4.4 collective-permute-start.1
  394.9 5.5 collective-permute-done
  400.3 4.5 collective-permute-start.3
  404.9 5.5 collective-permute-done.2
  410.3 1.0 collective-permute-start.4
  411.3 3.6 collective-permute-start.5
  414.9 5.5 collective-permute-done.4
  420.3 2.4 collective-permute-start.6
  422.8 2.1 collective-permute-start.7
  424.9 0.7 gather_fusion
  425.6 4.7 collective-permute-done.6
  430.3 3.8 collective-permute-start.8
  434.2 0.8 constant_dynamic-update-slice_fusion.14
  435.0 0.6 collective-permute-start.9
  435.6 0.8 constant_dynamic-update-slice_fusion.13
  436.5 3.8 collective-permute-done.8
  440.2 1.1 collective-permute-start.10
  441.4 0.8 constant_dynamic-update-slice_fusion.12
  442.2 0.8 constant_dynamic-update-slice_fusion.11
  443.0 0.9 constant_dynamic-update-slice_fusion.10
  443.9 3.4 collective-permute-start.11
  447.2 0.8 constant_dynamic-update-slice_fusion.9
  448.1 2.1 collective-permute-done.10
  450.2 1.1 collective-permute-start.12
  451.3 0.8 constant_dynamic-update-slice_fusion.8
  452.2 0.8 constant_dynamic-update-slice_fusion.7
  453.0 0.8 constant_dynamic-update-slice_fusion.6
  453.8 3.4 collective-permute-start.13
  457.2 0.8 constant_dynamic-update-slice_fusion.5
  458.0 2.1 collective-permute-done.12
  460.2 0.8 constant_dynamic-update-slice_fusion.4
  461.0 0.8 constant_dynamic-update-slice_fusion.3
  461.8 0.8 constant_dynamic-update-slice_fusion.2
  462.7 0.8 constant_dynamic-update-slice_fusion.1
  463.5 6.6 %collective-permute-done.14 = bf16[512,384]{1,0:T(8,128)(2,1)S(1)} collective-permute-done((bf16[512,384]{1,0:T(8,128)(2,1)S(1)}, bf16[512,384]{1,0:T(8,128)(2,1)S(1)}, u32[]{:S(2)}, u32[]{:S(2)}) %collective-permute-start.14) | collective-permute-done | bytes 393248 | tf_op jit(solution)/shard_map/ppermute | solution.py:27
  470.1 0.8 constant_dynamic-update-slice_fusion
  470.9 18.8 %fusion.22 = (f32[512]{0:T(512)S(1)}, f32[512,2048]{1,0:T(8,128)S(1)}) fusion(bf16[512,6144]{1,0:T(8,128)(2,1)} %constant_dynamic-update-slice_fusion, bf16[6144,2048]{1,0:T(8,128)(2,1)} %param.21), kind=kOutput, calls=%fused_computation.89 | convolution fusion | flops 12885950464 | bytes 35653632 | tf_op jit(solution)/shard_map/dot_general | solution.py:116
  489.7 1.4 select_reduce_fusion.1
  491.1 19.0 %all-gather.5 = f32[16,1,512]{2,1,0:T(1,128)S(1)} all-gather(f32[1,1,512]{2,1,0:T(1,128)S(1)} %bitcast.49), channel_id=4, replica_groups=mesh['groups'=2,'tensor'=16] {'tensor'}, dimensions={0}, use_global_device_ids=true | all-gather | bytes 34816 | tf_op jit(solution)/shard_map/all_gather | solution.py:43
  510.1 17.5 %all-gather.4 = f32[16,1,512]{2,1,0:T(1,128)S(1)} all-gather(f32[1,1,512]{2,1,0:T(1,128)S(1)} %bitcast.48), channel_id=3, replica_groups=mesh['groups'=2,'tensor'=16] {'tensor'}, dimensions={0}, use_global_device_ids=true | all-gather | bytes 34816 | tf_op jit(solution)/shard_map/all_gather | solution.py:43
  527.6 18.8 %all-gather.3 = f32[16,1,512]{2,1,0:T(1,128)S(1)} all-gather(f32[1,1,512]{2,1,0:T(1,128)S(1)} %bitcast.47), channel_id=2, replica_groups=mesh['groups'=2,'tensor'=16] {'tensor'}, dimensions={0}, use_global_device_ids=true | all-gather | bytes 34816 | tf_op jit(solution)/shard_map/all_gather | solution.py:43
  546.4 1.4 while.19
  (112 shorter events, 3.4 us)
Async XLA Ops:
  6.5 418.4 %copy-start = (s32[8]{0:T(128)S(1)}, s32[8]{0:T(128)}, u32[]{:S(2)}) copy-start(s32[8]{0:T(128)} %param.23) | copy-start | bytes 100
  6.5 101.9 %all-gather.8.cloned.1.call-start = ((), (), s32[]{:S(2)}) async-start(), calls=%async_computation.1 | async-start | bytes 6684672 | tf_op jit(solution)/shard_map/all_gather | solution.py:100
  45.3 307.8 %reduce-scatter.2.cloned.1.call-start = ((), (), s32[]{:S(2)}) async-start(), calls=%async_computation.2 | async-start | bytes 13369344 | tf_op jit(solution)/shard_map/reduce_scatter | solution.py:111
  123.9 16.5 %copy-start.2 = (bf16[384,6144]{1,0:T(8,128)(2,1)S(1)}, bf16[384,6144]{1,0:T(8,128)(2,1)}, u32[]{:S(2)}) copy-start(bf16[384,6144]{1,0:T(8,128)(2,1)} %gather_fusion.1) | copy-start | bytes 14155780
  219.9 0.7 copy-start.5
  219.9 133.1 %copy-start.1 = (bf16[512,384]{1,0:T(8,128)(2,1)S(1)}, bf16[512,384]{1,0:T(8,128)(2,1)}, u32[]{:S(2)}) copy-start(bf16[512,384]{1,0:T(8,128)(2,1)} %param.13) | copy-start | bytes 1179652
  219.9 214.2 %copy-start.4 = (s32[512]{0:T(512)S(1)}, s32[512]{0:T(512)}, u32[]{:S(2)}) copy-start(s32[512]{0:T(512)} %param.22) | copy-start | bytes 6148
  353.0 36.4 %copy-start.3 = (f32[512,384]{1,0:T(8,128)S(1)}, f32[512,384]{1,0:T(8,128)}, u32[]{:S(2)}) copy-start(f32[512,384]{1,0:T(8,128)} %reduce-scatter.2.cloned.1.call-done) | copy-start | bytes 2359300
  390.4 9.9 %collective-permute-start = (bf16[512,384]{1,0:T(8,128)(2,1)S(1)}, bf16[512,384]{1,0:T(8,128)(2,1)S(1)}, u32[]{:S(2)}, u32[]{:S(2)}) collective-permute-start(bf16[512,384]{1,0:T(8,128)(2,1)S(1)} %get-tuple-element.207), channel_id=1, source_target_pairs={{0,1},{1,2},{2,3},{3,4},{4,5},{5,6},{6,7},{7,8},{8,9},{9,10},{10,1... | collective-permute-start | bytes 1179656 | tf_op jit(solution)/shard_map/ppermute | solution.py:27
  390.4 9.9 %collective-permute-start.1 = (bf16[512,384]{1,0:T(8,128)(2,1)S(1)}, bf16[512,384]{1,0:T(8,128)(2,1)S(1)}, u32[]{:S(2)}, u32[]{:S(2)}) collective-permute-start(bf16[512,384]{1,0:T(8,128)(2,1)S(1)} %get-tuple-element.207), channel_id=1, source_target_pairs={{0,15},{1,0},{2,1},{3,2},{4,3},{5,4},{6,5},{7,6},{8,7},{9,8},{10,9... | collective-permute-start | bytes 1179656 | tf_op jit(solution)/shard_map/ppermute | solution.py:34
  400.3 10.0 %collective-permute-start.2 = (bf16[512,384]{1,0:T(8,128)(2,1)S(1)}, bf16[512,384]{1,0:T(8,128)(2,1)S(1)}, u32[]{:S(2)}, u32[]{:S(2)}) collective-permute-start(bf16[512,384]{1,0:T(8,128)(2,1)S(1)} %collective-permute-done), channel_id=1, source_target_pairs={{0,1},{1,2},{2,3},{3,4},{4,5},{5,6},{6,7},{7,8},{8,9},{9,10},{10,1... | collective-permute-start | bytes 1179656 | tf_op jit(solution)/shard_map/ppermute | solution.py:27
  400.3 11.0 %collective-permute-start.3 = (bf16[512,384]{1,0:T(8,128)(2,1)S(1)}, bf16[512,384]{1,0:T(8,128)(2,1)S(1)}, u32[]{:S(2)}, u32[]{:S(2)}) collective-permute-start(bf16[512,384]{1,0:T(8,128)(2,1)S(1)} %collective-permute-done.1), channel_id=1, source_target_pairs={{0,15},{1,0},{2,1},{3,2},{4,3},{5,4},{6,5},{7,6},{8,7},{9,8},{10,9... | collective-permute-start | bytes 1179656 | tf_op jit(solution)/shard_map/ppermute | solution.py:34
  410.3 10.0 %collective-permute-start.4 = (bf16[512,384]{1,0:T(8,128)(2,1)S(1)}, bf16[512,384]{1,0:T(8,128)(2,1)S(1)}, u32[]{:S(2)}, u32[]{:S(2)}) collective-permute-start(bf16[512,384]{1,0:T(8,128)(2,1)S(1)} %collective-permute-done.2), channel_id=1, source_target_pairs={{0,1},{1,2},{2,3},{3,4},{4,5},{5,6},{6,7},{7,8},{8,9},{9,10},{10,1... | collective-permute-start | bytes 1179656 | tf_op jit(solution)/shard_map/ppermute | solution.py:27
  411.3 11.4 %collective-permute-start.5 = (bf16[512,384]{1,0:T(8,128)(2,1)S(1)}, bf16[512,384]{1,0:T(8,128)(2,1)S(1)}, u32[]{:S(2)}, u32[]{:S(2)}) collective-permute-start(bf16[512,384]{1,0:T(8,128)(2,1)S(1)} %collective-permute-done.3), channel_id=1, source_target_pairs={{0,15},{1,0},{2,1},{3,2},{4,3},{5,4},{6,5},{7,6},{8,7},{9,8},{10,9... | collective-permute-start | bytes 1179656 | tf_op jit(solution)/shard_map/ppermute | solution.py:34
  420.3 10.0 %collective-permute-start.6 = (bf16[512,384]{1,0:T(8,128)(2,1)S(1)}, bf16[512,384]{1,0:T(8,128)(2,1)S(1)}, u32[]{:S(2)}, u32[]{:S(2)}) collective-permute-start(bf16[512,384]{1,0:T(8,128)(2,1)S(1)} %collective-permute-done.4), channel_id=1, source_target_pairs={{0,1},{1,2},{2,3},{3,4},{4,5},{5,6},{6,7},{7,8},{8,9},{9,10},{10,1... | collective-permute-start | bytes 1179656 | tf_op jit(solution)/shard_map/ppermute | solution.py:27
  422.8 12.2 %collective-permute-start.7 = (bf16[512,384]{1,0:T(8,128)(2,1)S(1)}, bf16[512,384]{1,0:T(8,128)(2,1)S(1)}, u32[]{:S(2)}, u32[]{:S(2)}) collective-permute-start(bf16[512,384]{1,0:T(8,128)(2,1)S(1)} %collective-permute-done.5), channel_id=1, source_target_pairs={{0,15},{1,0},{2,1},{3,2},{4,3},{5,4},{6,5},{7,6},{8,7},{9,8},{10,9... | collective-permute-start | bytes 1179656 | tf_op jit(solution)/shard_map/ppermute | solution.py:34
  430.3 9.9 %collective-permute-start.8 = (bf16[512,384]{1,0:T(8,128)(2,1)S(1)}, bf16[512,384]{1,0:T(8,128)(2,1)S(1)}, u32[]{:S(2)}, u32[]{:S(2)}) collective-permute-start(bf16[512,384]{1,0:T(8,128)(2,1)S(1)} %collective-permute-done.6), channel_id=1, source_target_pairs={{0,1},{1,2},{2,3},{3,4},{4,5},{5,6},{6,7},{7,8},{8,9},{9,10},{10,1... | collective-permute-start | bytes 1179656 | tf_op jit(solution)/shard_map/ppermute | solution.py:27
  435.0 8.9 %collective-permute-start.9 = (bf16[512,384]{1,0:T(8,128)(2,1)S(1)}, bf16[512,384]{1,0:T(8,128)(2,1)S(1)}, u32[]{:S(2)}, u32[]{:S(2)}) collective-permute-start(bf16[512,384]{1,0:T(8,128)(2,1)S(1)} %collective-permute-done.7), channel_id=1, source_target_pairs={{0,15},{1,0},{2,1},{3,2},{4,3},{5,4},{6,5},{7,6},{8,7},{9,8},{10,9... | collective-permute-start | bytes 1179656 | tf_op jit(solution)/shard_map/ppermute | solution.py:34
  440.2 10.0 %collective-permute-start.10 = (bf16[512,384]{1,0:T(8,128)(2,1)S(1)}, bf16[512,384]{1,0:T(8,128)(2,1)S(1)}, u32[]{:S(2)}, u32[]{:S(2)}) collective-permute-start(bf16[512,384]{1,0:T(8,128)(2,1)S(1)} %collective-permute-done.8), channel_id=1, source_target_pairs={{0,1},{1,2},{2,3},{3,4},{4,5},{5,6},{6,7},{7,8},{8,9},{9,10},{10,1... | collective-permute-start | bytes 1179656 | tf_op jit(solution)/shard_map/ppermute | solution.py:27
  443.9 10.0 %collective-permute-start.11 = (bf16[512,384]{1,0:T(8,128)(2,1)S(1)}, bf16[512,384]{1,0:T(8,128)(2,1)S(1)}, u32[]{:S(2)}, u32[]{:S(2)}) collective-permute-start(bf16[512,384]{1,0:T(8,128)(2,1)S(1)} %collective-permute-done.9), channel_id=1, source_target_pairs={{0,15},{1,0},{2,1},{3,2},{4,3},{5,4},{6,5},{7,6},{8,7},{9,8},{10,9... | collective-permute-start | bytes 1179656 | tf_op jit(solution)/shard_map/ppermute | solution.py:34
  450.2 10.0 %collective-permute-start.12 = (bf16[512,384]{1,0:T(8,128)(2,1)S(1)}, bf16[512,384]{1,0:T(8,128)(2,1)S(1)}, u32[]{:S(2)}, u32[]{:S(2)}) collective-permute-start(bf16[512,384]{1,0:T(8,128)(2,1)S(1)} %collective-permute-done.10), channel_id=1, source_target_pairs={{0,1},{1,2},{2,3},{3,4},{4,5},{5,6},{6,7},{7,8},{8,9},{9,10},{10,1... | collective-permute-start | bytes 1179656 | tf_op jit(solution)/shard_map/ppermute | solution.py:27
  453.8 8.9 %collective-permute-start.13 = (bf16[512,384]{1,0:T(8,128)(2,1)S(1)}, bf16[512,384]{1,0:T(8,128)(2,1)S(1)}, u32[]{:S(2)}, u32[]{:S(2)}) collective-permute-start(bf16[512,384]{1,0:T(8,128)(2,1)S(1)} %collective-permute-done.11), channel_id=1, source_target_pairs={{0,15},{1,0},{2,1},{3,2},{4,3},{5,4},{6,5},{7,6},{8,7},{9,8},{10,9... | collective-permute-start | bytes 1179656 | tf_op jit(solution)/shard_map/ppermute | solution.py:34
  460.2 9.9 %collective-permute-start.14 = (bf16[512,384]{1,0:T(8,128)(2,1)S(1)}, bf16[512,384]{1,0:T(8,128)(2,1)S(1)}, u32[]{:S(2)}, u32[]{:S(2)}) collective-permute-start(bf16[512,384]{1,0:T(8,128)(2,1)S(1)} %collective-permute-done.12), channel_id=1, source_target_pairs={{0,1},{1,2},{2,3},{3,4},{4,5},{5,6},{6,7},{7,8},{8,9},{9,10},{10,1... | collective-permute-start | bytes 1179656 | tf_op jit(solution)/shard_map/ppermute | solution.py:27
Sparse Core Ops, SparseCore 0:
  45.4 62.9 all-gather.7
  220.1 132.9 reduce-scatter.1
